TPU v7x, 256 devices: a whole 4x4x8 slice. The times are simulated.
256 devices in a mesh: sx: 4 (over x_hi, core), sy: 32 (over y, z), ta: 2 (over x_lo).
Axes of the slice: x: 4 (x_hi: 2, x_lo: 2; x = x_hi * 2 + x_lo), y: 4, z: 8, core: 2. Of those that a mesh axis runs over, the one named last changes fastest.
Arguments:
- forcing: float32 [64, 128, 4096], P('ta', 'sx', 'sy'), may hold values from -12 to 12
- react: float32 [128, 4096], P('sx', 'sy'), may hold values from 0.05 to 1
- initial: float32 [128, 4096], P('sx', 'sy'), may hold values from -8 to 8
Outputs:
- solution: float32 [64, 128, 4096], P('ta', 'sx', 'sy')
- square_means: float32 [3], replicated
All inputs are finite; a program needn't handle non-finite values.
Results may differ from a plain program's by a relative error of at most 0.0001.
Values sent between devices are 32-bit elements; how exact they have to be, the bound alone decides.
A program may use at most 64 MiB of HBM per device.

v0:
```python
import functools

import jax
import jax.numpy as jnp
from jax import lax
from jax.experimental import pallas as pl
from jax.experimental.pallas import tpu as pltpu
from jax.sharding import PartitionSpec as P

SWEEPS = 8
ALPHA = 0.1
STEP = 2.0
CORNER = ALPHA / STEP
OWN = 16
HALO = 16
WIDE = OWN + 2 * HALO
LINE = 8
MESH = pl.DeviceIdType.MESH


def iota(axis):
    return lax.broadcasted_iota(jnp.int32, (8, 128), axis)


def place_of(p):
    return 2 * (p // 4) + p % 2, (p // 2) % 2


def swap_groups(v):
    lane = iota(1)
    low = lane < 64
    even = (lane // 32) % 2 == 0
    a = [
        jnp.where(low, v[0], pltpu.roll(v[2], 64, 1)),
        jnp.where(low, v[1], pltpu.roll(v[3], 64, 1)),
        jnp.where(low, pltpu.roll(v[0], 64, 1), v[2]),
        jnp.where(low, pltpu.roll(v[1], 64, 1), v[3]),
    ]
    return [
        jnp.where(even, a[0], pltpu.roll(a[1], 32, 1)),
        jnp.where(even, pltpu.roll(a[0], 96, 1), a[1]),
        jnp.where(even, a[2], pltpu.roll(a[3], 32, 1)),
        jnp.where(even, pltpu.roll(a[2], 96, 1), a[3]),
    ]


def kernel(ny, nz, f, react, init, out, stat, S, rcv, tmp, rsend, rrecv, rext, Rx, CR, U, CF, E,
           M, O, redx, redy, redz, a_s, a_r, c_s, c_r, h_s, h_r, o_s, o_r, x_s, x_r, y_s, y_r,
           z_s, z_r, l_s):
    sx, sy, ta = lax.axis_index("sx"), lax.axis_index("sy"), lax.axis_index("ta")
    nsy = ny * nz
    p = 4 * (sx // 2) + 2 * ta + sx % 2
    odd = sy % 2

    def slice_of(q):
        return q + odd * (7 - 2 * q)

    d = slice_of(p)

    def in_line(q):
        a, b = place_of(q)
        return {"sx": a, "sy": sy, "ta": b}

    def beside(step):
        q = d + step
        inside = jnp.logical_and(q >= 0, q <= 7)
        s = jnp.where(inside, sy, lax.rem(sy + step + nsy, nsy))
        e = jnp.where(inside, slice_of(jnp.clip(q, 0, 7)), p)
        a, b = place_of(e)
        return {"sx": a, "sy": s, "ta": b}

    def in_y(k):
        return {"sx": sx, "sy": lax.rem(sy + nz * k, nsy), "ta": ta}

    def in_z(k):
        z = lax.rem(sy, nz)
        return {"sx": sx, "sy": sy - z + lax.rem(z + k, nz), "ta": ta}

    left, right = beside(-1), beside(1)
    barrier = pltpu.get_barrier_semaphore()
    peers = [in_line(lax.rem(p + k, LINE)) for k in range(1, LINE)]
    peers += [left, right]
    peers += [in_y(k) for k in range(1, ny)]
    peers += [in_z(k) for k in range(1, nz)]
    for peer in peers:
        pl.semaphore_signal(barrier, inc=1, device_id=peer, device_id_type=MESH)

    def remote(src, dst, s_sem, r_sem, peer):
        return pltpu.make_async_remote_copy(
            src_ref=src, dst_ref=dst, send_sem=s_sem, recv_sem=r_sem, device_id=peer,
            device_id_type=MESH,
        )

    tmp[...] = jnp.zeros_like(tmp)
    tmp[pl.ds(pl.multiple_of(sx * 32, 32), 32), :] = react[...]
    rsend[...] = tmp[...].T
    opening = jnp.where(ta == 0, 1.0 / STEP, 0.0)
    for m in range(8):
        b = m % 4
        q = lax.rem(m // 4 + ta, 2)
        planes = [f[8 * b + 2 * g + q] for g in range(4)]
        if m == 0:
            planes[0] = planes[0] + opening * init[...]
        S[pl.ds(m, 128, stride=8), :] = jnp.concatenate(planes, axis=0).T

    pl.semaphore_wait(barrier, len(peers))

    copies_c = []
    for k in range(1, 4):
        to = lax.rem(sx + k, 4)
        q = 4 * (to // 2) + 2 * ta + to % 2
        rows = pl.ds(pl.multiple_of(slice_of(q) * OWN, OWN), OWN)
        c = remote(rsend.at[rows], rrecv.at[sx], c_s.at[k], c_r.at[k],
                   {"sx": to, "sy": sy, "ta": ta})
        c.start()
        copies_c.append(c)
    copies_a = []
    for k in range(1, LINE):
        q = lax.rem(p + k, LINE)
        rows = pl.ds(pl.multiple_of(slice_of(q) * 128, 128), 128)
        c = remote(S.at[rows], rcv.at[p], a_s.at[k], a_r.at[k], in_line(q))
        c.start()
        copies_a.append(c)
    mine = pltpu.make_async_copy(S.at[pl.ds(pl.multiple_of(d * 128, 128), 128)], rcv.at[p],
                                 l_s.at[0])
    mine.start()
    rrecv[sx] = rsend[pl.ds(pl.multiple_of(d * OWN, OWN), OWN), :]
    for c in copies_c:
        c.wait()
    rext[pl.ds(HALO, OWN), :] = (rrecv[0] + rrecv[1]) + (rrecv[2] + rrecv[3])
    halo_c = [
        remote(rext.at[pl.ds(HALO, OWN)], rext.at[pl.ds(HALO + OWN, HALO)], h_s.at[0], h_r.at[0],
               left),
        remote(rext.at[pl.ds(HALO, OWN)], rext.at[pl.ds(0, HALO)], h_s.at[1], h_r.at[1], right),
    ]
    for c in halo_c:
        c.start()

    sub = iota(0)
    lane = iota(1)
    first = sub == 0

    def coefficients(col, inside):
        r = jnp.broadcast_to(rext[pl.ds(col, 1), :], (8, 128))
        c = inside / (1.0 / STEP + 4.0 + r)
        cp = c / STEP
        q2 = cp * cp
        q4 = q2 * q2
        q = q4 * q4
        qq = q * q
        qqqq = qq * qq
        CF[col, 0] = c
        CF[col, 1] = cp
        CF[col, 2] = jnp.where(sub < 1, ALPHA * q, q)
        CF[col, 3] = jnp.where(sub < 2, ALPHA * qq, qq)
        CF[col, 4] = jnp.where(sub < 4, ALPHA * qqqq, qqqq)
        ks = cp / (1.0 - ALPHA * (qqqq * qqqq))
        CF[col, 5] = jnp.where(first, ALPHA * ks, ks)

    def solve(g, col):
        cp = CF[col, 1]
        z = [g[0]]
        for l in range(1, 8):
            z.append(g[l] + cp * z[-1])
        a = z[7]
        a = a + CF[col, 2] * pltpu.roll(a, 1, 0)
        a = a + CF[col, 3] * pltpu.roll(a, 2, 0)
        a = a + CF[col, 4] * pltpu.roll(a, 4, 0)
        s = CF[col, 5] * pltpu.roll(a, 1, 0)
        done = []
        for l in range(8):
            done.append(z[l] + s)
            if l < 7:
                s = s * cp
        return done

    def part(l):
        return pl.ds(8 * l, 8)

    def rows_beside(v):
        return (jnp.where(lane == 0, 0.0, pltpu.roll(v, 1, 1))
                + jnp.where(lane == 127, 0.0, pltpu.roll(v, 127, 1)))

    def first_sweep(col, inside):
        coefficients(col, inside)
        c = CF[col, 0]
        g = []
        for l in range(8):
            v = c * Rx[col, part(l), :]
            CR[col, part(l), :] = v
            g.append(v)
        u = solve(g, col)
        for l in range(8):
            U[0, col, part(l), :] = u[l]

    def spread(lo, hi, fn):
        def step(i, carry):
            fn(lo + i)
            return carry

        lax.fori_loop(0, hi - lo, step, 0)

    mine.wait()
    for c in copies_a:
        c.wait()

    def unpack(col, acc):
        rows = pl.ds(pl.multiple_of(8 * col, 8), 8)
        w = []
        for t in range(2):
            v = [rcv[4 * (s // 2) + 2 * t + s % 2, rows, :] for s in range(4)]
            w.append(swap_groups(v))
        for g in range(4):
            even = jnp.where(sub < 4, w[0][g], w[1][g])
            other = pltpu.roll(jnp.where(sub < 4, w[1][g], w[0][g]), 4, 0)
            Rx[HALO + col, part(2 * g), :] = even
            Rx[HALO + col, part(2 * g + 1), :] = other
            acc = acc + even * even + other * other
        return acc

    acc0 = lax.fori_loop(0, OWN, unpack, jnp.zeros((8, 128), jnp.float32))
    halo_r = [
        remote(Rx.at[pl.ds(HALO, OWN)], Rx.at[pl.ds(HALO + OWN, HALO)], h_s.at[2], h_r.at[2],
               left),
        remote(Rx.at[pl.ds(HALO, OWN)], Rx.at[pl.ds(0, HALO)], h_s.at[3], h_r.at[3], right),
    ]
    for c in halo_r:
        c.start()
    spread(HALO, HALO + OWN, lambda col: first_sweep(col, 1.0))
    for c in halo_c:
        c.wait()
    for c in halo_r:
        c.wait()
    at_start = jnp.logical_and(sy == 0, d == 0)
    at_end = jnp.logical_and(sy == nsy - 1, d == 7)
    in_left = jnp.where(at_start, 0.0, 1.0)
    in_right = jnp.where(at_end, 0.0, 1.0)
    spread(0, HALO, lambda col: first_sweep(col, in_left))
    spread(HALO + OWN, WIDE, lambda col: first_sweep(col, in_right))

    def sweep(j, carry):
        now, later = lax.rem(j, 2), lax.rem(j + 1, 2)

        def one(col):
            c = CF[col, 0]
            g = []
            for l in range(8):
                v = U[now, col, part(l), :]
                n = (U[now, col - 1, part(l), :] + U[now, col + 1, part(l), :]) + rows_beside(v)
                g.append(CR[col, part(l), :] + c * n)
            u = solve(g, col)
            for l in range(8):
                U[later, col, part(l), :] = u[l]

        def step(i, carry):
            one(j + 1 + 2 * i)
            one(j + 2 + 2 * i)
            return carry

        lax.fori_loop(0, WIDE // 2 - 1 - j, step, 0)
        return carry

    def left_over(now, last):
        def step(i, acc):
            col = HALO + i

            def change(k, l):
                return U[now, k, part(l), :] - U[1 - now, k, part(l), :]

            for l in range(8):
                r = change(col - 1, l) + change(col + 1, l) + rows_beside(change(col, l))
                if l == 0:
                    e = CORNER * pltpu.roll(U[now, col, part(7), :], 1, 0)
                    e = jnp.where(first, e, 0.0)
                    r = r + (E[col] - e) if last else r - e
                acc = acc + r * r
            return acc

        return lax.fori_loop(0, OWN, step, jnp.zeros((8, 128), jnp.float32))

    lax.fori_loop(0, SWEEPS - 1, sweep, 0)
    acc1 = left_over((SWEEPS - 1) % 2, False)

    def corner(col):
        e = CORNER * pltpu.roll(U[(SWEEPS - 1) % 2, col, part(7), :], 1, 0)
        e = jnp.where(first, e, 0.0)
        E[col] = e
        CR[col, part(0), :] = CR[col, part(0), :] - CF[col, 0] * e

    spread(SWEEPS - 1, WIDE - SWEEPS + 1, corner)
    lax.fori_loop(SWEEPS - 1, 2 * SWEEPS - 1, sweep, 0)
    acc2 = left_over((2 * SWEEPS - 1) % 2, True)

    def total(v):
        return jnp.sum(v, axis=0, keepdims=True)

    redx[p] = jnp.where(sub == 0, total(acc0), jnp.where(sub == 1, total(acc1), jnp.where(
        sub == 2, total(acc2), 0.0)))
    copies_x = []
    for k in range(1, LINE):
        c = remote(redx.at[p], redx.at[p], x_s.at[k], x_r.at[k], in_line(lax.rem(p + k, LINE)))
        c.start()
        copies_x.append(c)

    ended = (2 * SWEEPS - 1) % 2

    def pack(col, carry):
        rows = pl.ds(pl.multiple_of(8 * col, 8), 8)
        w = [[], []]
        for g in range(4):
            even = U[ended, HALO + col, part(2 * g), :]
            other = pltpu.roll(U[ended, HALO + col, part(2 * g + 1), :], 4, 0)
            w[0].append(jnp.where(sub < 4, even, other))
            w[1].append(jnp.where(sub < 4, other, even))
        for t in range(2):
            v = swap_groups(w[t])
            for s in range(4):
                M[4 * (s // 2) + 2 * t + s % 2, rows, :] = v[s]
        return carry

    lax.fori_loop(0, OWN, pack, 0)
    slot = pl.ds(pl.multiple_of(d * 128, 128), 128)
    copies_o = []
    for k in range(1, LINE):
        q = lax.rem(p + k, LINE)
        c = remote(M.at[q], O.at[slot], o_s.at[k], o_r.at[k], in_line(q))
        c.start()
        copies_o.append(c)
    mine = pltpu.make_async_copy(M.at[p], O.at[slot], l_s.at[1])
    mine.start()

    for c in copies_x:
        c.wait()
    sums = redx[0]
    for k in range(1, LINE):
        sums = sums + redx[k]
    if ny > 1:
        y = sy // nz
        redy[y] = sums
        copies_y = []
        for k in range(1, ny):
            c = remote(redy.at[y], redy.at[y], y_s.at[k], y_r.at[k], in_y(k))
            c.start()
            copies_y.append(c)
        for c in copies_y:
            c.wait()
        sums = redy[0]
        for k in range(1, ny):
            sums = sums + redy[k]
    if nz > 1:
        z = lax.rem(sy, nz)
        redz[z] = sums
        copies_z = []
        for k in range(1, nz):
            c = remote(redz.at[z], redz.at[z], z_s.at[k], z_r.at[k], in_z(k))
            c.start()
            copies_z.append(c)

    mine.wait()
    for c in copies_o:
        c.wait()
    for m in range(8):
        b = m % 4
        q = lax.rem(m // 4 + ta, 2)
        x = O[pl.ds(m, 128, stride=8), :].T
        for g in range(4):
            out[8 * b + 2 * g + q] = x[32 * g:32 * g + 32, :]

    if nz > 1:
        for c in copies_z:
            c.wait()
        sums = redz[0]
        for k in range(1, nz):
            sums = sums + redz[k]
    cells = 64.0 * 128.0 * (128.0 * nsy)
    for i in range(3):
        stat[i] = jnp.sum(sums[i:i + 1, :]) / cells


def solution(mesh):
    nsy = mesh.shape["sy"]
    ny, nz = (4, 8) if nsy == 32 else (2, nsy // 2)

    def step(forcing, react, initial):
        vmem = pl.BlockSpec(memory_space=pltpu.VMEM)
        dma = pltpu.SemaphoreType.DMA
        f32 = jnp.float32
        return pl.pallas_call(
            functools.partial(kernel, ny, nz),
            out_shape=(
                jax.ShapeDtypeStruct((32, 32, 128), f32),
                jax.ShapeDtypeStruct((3,), f32),
            ),
            in_specs=[vmem] * 3,
            out_specs=(vmem, pl.BlockSpec(memory_space=pltpu.SMEM)),
            scratch_shapes=[
                pltpu.VMEM((1024, 128), f32),
                pltpu.VMEM((8, 128, 128), f32),
                pltpu.VMEM((128, 128), f32),
                pltpu.VMEM((128, 128), f32),
                pltpu.VMEM((4, OWN, 128), f32),
                pltpu.VMEM((WIDE, 128), f32),
                pltpu.VMEM((WIDE, 64, 128), f32),
                pltpu.VMEM((WIDE, 64, 128), f32),
                pltpu.VMEM((2, WIDE, 64, 128), f32),
                pltpu.VMEM((WIDE, 6, 8, 128), f32),
                pltpu.VMEM((WIDE, 8, 128), f32),
                pltpu.VMEM((8, 128, 128), f32),
                pltpu.VMEM((1024, 128), f32),
                pltpu.VMEM((LINE, 8, 128), f32),
                pltpu.VMEM((max(ny, 2), 8, 128), f32),
                pltpu.VMEM((max(nz, 2), 8, 128), f32),
                dma((8,)), dma((8,)), dma((4,)), dma((4,)), dma((4,)), dma((4,)),
                dma((8,)), dma((8,)), dma((8,)), dma((8,)), dma((max(ny, 2),)),
                dma((max(ny, 2),)), dma((max(nz, 2),)), dma((max(nz, 2),)), dma((2,)),
            ],
            compiler_params=pltpu.CompilerParams(
                collective_id=0, has_side_effects=True, vmem_limit_bytes=48 << 20
            ),
        )(forcing, react, initial)

    placed = (P("ta", "sx", "sy"), P("sx", "sy"), P("sx", "sy"))
    return jax.shard_map(
        step, mesh=mesh, in_specs=placed, out_specs=(P("ta", "sx", "sy"), P(None)),
        check_vma=False,
    )
```

profile of v0, /device:TPU:6, one launch (start us, length us, event | category | flops | bytes accessed | tf_op | source)
XLA Modules:
  0.0 102.1 jit_solution(10049894241743470643)
XLA Ops:
  0.6 0.0 copy-start
  0.6 1.0 %copy-done = f32[32,32,128]{2,1,0:T(8,128)S(1)} copy-done((f32[32,32,128]{2,1,0:T(8,128)S(1)}, f32[32,32,128]{2,1,0:T(8,128)}, u32[]{:S(2)}) %copy-start) | copy-done | bytes 524312
  1.7 0.0 copy-start.1
  1.7 0.7 copy-done.1
  2.4 0.0 copy-start.2
  2.4 0.7 copy-done.2
  3.1 97.7 %shard_map.50 = (f32[32,32,128]{2,1,0:T(8,128)S(1)}, f32[3]{0:T(128)S(1)}) custom-call(f32[32,32,128]{2,1,0:T(8,128)S(1)} %copy-done, f32[32,128]{1,0:T(8,128)S(1)} %copy-done.1, f32[32,128]{1,0:T(8,128)S(1)} %copy-done.2), custom_call_target="tpu_custom_call" | custom-call | tf_op jit(solution)/shard_map/pallas_call | solution.py:388
  100.8 0.8 copy.7
  101.6 0.5 copy.8
Async XLA Ops:
  0.6 1.0 %copy-start = (f32[32,32,128]{2,1,0:T(8,128)S(1)}, f32[32,32,128]{2,1,0:T(8,128)}, u32[]{:S(2)}) copy-start(f32[32,32,128]{2,1,0:T(8,128)} %f.1) | copy-start | bytes 1572868
  1.7 0.7 copy-start.1
  2.4 0.7 copy-start.2
where the time goes:
time: 103 us; the launch traced here: 102 us
  Pallas kernels  97.7 us (95%)
  local copies, waits for them, and re-layouts  3.78 us (4%)
    pallas_call x1, Pallas kernels, step(): pl.pallas_call(functools.partial(kernel, ny, nz), out_shape=(jax.ShapeDty...  97.7 us
    unnamed x8, local copies, waits for them, and re-layouts  3.78 us

commit v1 on v0

v1 whole, which is shorter than its diff:
```python
import functools

import jax
import jax.numpy as jnp
from jax import lax
from jax.experimental import pallas as pl
from jax.experimental.pallas import tpu as pltpu
from jax.sharding import PartitionSpec as P

SWEEPS = 8
ALPHA = 0.1
STEP = 2.0
CORNER = ALPHA / STEP
OWN = 16
HALO = 8
WIDE = OWN + 2 * HALO
ENDS = HALO + OWN
LINE = 8
UNROLL = 8
MESH = pl.DeviceIdType.MESH


def iota(axis):
    return lax.broadcasted_iota(jnp.int32, (8, 128), axis)


def place_of(p):
    return 2 * (p // 4) + p % 2, (p // 2) % 2


def swap_groups(v):
    lane = iota(1)
    low = lane < 64
    even = (lane // 32) % 2 == 0
    a = [
        jnp.where(low, v[0], pltpu.roll(v[2], 64, 1)),
        jnp.where(low, v[1], pltpu.roll(v[3], 64, 1)),
        jnp.where(low, pltpu.roll(v[0], 64, 1), v[2]),
        jnp.where(low, pltpu.roll(v[1], 64, 1), v[3]),
    ]
    return [
        jnp.where(even, a[0], pltpu.roll(a[1], 32, 1)),
        jnp.where(even, pltpu.roll(a[0], 96, 1), a[1]),
        jnp.where(even, a[2], pltpu.roll(a[3], 32, 1)),
        jnp.where(even, pltpu.roll(a[2], 96, 1), a[3]),
    ]


def part(l):
    return pl.ds(8 * l, 8)


def kernel(ny, nz, f_hbm, react_hbm, init_hbm, out, stat, f, react, init, S, rcv, tmp, rsend, rrecv,
           rext, Rx, CR, U0, U1, V0, NB, CL, PW, KS, E, M, O, redx, redy, redz, a_s, a_r, c_s, c_r,
           h_s, h_r, o_s, o_r, x_s, x_r, y_s, y_r, z_s, z_r, l_s):
    sx, sy, ta = lax.axis_index("sx"), lax.axis_index("sy"), lax.axis_index("ta")
    nsy = ny * nz
    p = 4 * (sx // 2) + 2 * ta + sx % 2
    odd = sy % 2

    def slice_of(q):
        return q + odd * (7 - 2 * q)

    d = slice_of(p)

    def in_line(q):
        a, b = place_of(q)
        return {"sx": a, "sy": sy, "ta": b}

    def beside(step):
        q = d + step
        inside = jnp.logical_and(q >= 0, q <= 7)
        s = jnp.where(inside, sy, lax.rem(sy + step + nsy, nsy))
        e = jnp.where(inside, slice_of(jnp.clip(q, 0, 7)), p)
        a, b = place_of(e)
        return {"sx": a, "sy": s, "ta": b}

    def in_y(k):
        return {"sx": sx, "sy": lax.rem(sy + nz * k, nsy), "ta": ta}

    def in_z(k):
        z = lax.rem(sy, nz)
        return {"sx": sx, "sy": sy - z + lax.rem(z + k, nz), "ta": ta}

    left, right = beside(-1), beside(1)
    inputs = [
        pltpu.make_async_copy(react_hbm, react, l_s.at[2]),
        pltpu.make_async_copy(init_hbm, init, l_s.at[3]),
        pltpu.make_async_copy(f_hbm, f, l_s.at[4]),
    ]
    for c in inputs:
        c.start()
    barrier = pltpu.get_barrier_semaphore()
    peers = [in_line(lax.rem(p + k, LINE)) for k in range(1, LINE)]
    peers += [left, right]
    peers += [in_y(k) for k in range(1, ny)]
    peers += [in_z(k) for k in range(1, nz)]
    for peer in peers:
        pl.semaphore_signal(barrier, inc=1, device_id=peer, device_id_type=MESH)

    def remote(src, dst, s_sem, r_sem, peer):
        return pltpu.make_async_remote_copy(
            src_ref=src, dst_ref=dst, send_sem=s_sem, recv_sem=r_sem, device_id=peer,
            device_id_type=MESH,
        )

    tmp[...] = jnp.zeros_like(tmp)
    inputs[0].wait()
    tmp[pl.ds(pl.multiple_of(sx * 32, 32), 32), :] = react[...]
    rsend[...] = tmp[...].T
    inputs[1].wait()
    inputs[2].wait()
    opening = jnp.where(ta == 0, 1.0 / STEP, 0.0)
    for m in range(8):
        b = m % 4
        q = lax.rem(m // 4 + ta, 2)
        planes = [f[8 * b + 2 * g + q] for g in range(4)]
        if m == 0:
            planes[0] = planes[0] + opening * init[...]
        S[pl.ds(m, 128, stride=8), :] = jnp.concatenate(planes, axis=0).T

    pl.semaphore_wait(barrier, len(peers))

    copies_c = []
    for k in range(1, 4):
        to = lax.rem(sx + k, 4)
        q = 4 * (to // 2) + 2 * ta + to % 2
        rows = pl.ds(pl.multiple_of(slice_of(q) * OWN, OWN), OWN)
        c = remote(rsend.at[rows], rrecv.at[sx], c_s.at[k], c_r.at[k],
                   {"sx": to, "sy": sy, "ta": ta})
        c.start()
        copies_c.append(c)
    copies_a = []
    for k in range(1, LINE):
        q = lax.rem(p + k, LINE)
        rows = pl.ds(pl.multiple_of(slice_of(q) * 128, 128), 128)
        c = remote(S.at[rows], rcv.at[p], a_s.at[k], a_r.at[k], in_line(q))
        c.start()
        copies_a.append(c)
    mine = pltpu.make_async_copy(S.at[pl.ds(pl.multiple_of(d * 128, 128), 128)], rcv.at[p],
                                 l_s.at[0])
    mine.start()
    rrecv[sx] = rsend[pl.ds(pl.multiple_of(d * OWN, OWN), OWN), :]
    for c in copies_c:
        c.wait()
    rext[pl.ds(HALO, OWN), :] = (rrecv[0] + rrecv[1]) + (rrecv[2] + rrecv[3])

    def edges(src, left_dst, right_dst, k):
        return (
            remote(src.at[pl.ds(HALO, HALO)], left_dst, h_s.at[2 * k], h_r.at[2 * k], left),
            remote(src.at[pl.ds(OWN, HALO)], right_dst, h_s.at[2 * k + 1], h_r.at[2 * k + 1],
                   right),
        )

    def halos(ref, k):
        return edges(ref, ref.at[pl.ds(ENDS, HALO)], ref.at[pl.ds(0, HALO)], k)

    halo_c = halos(rext, 0)
    for c in halo_c:
        c.start()

    sub = iota(0)
    lane = iota(1)
    first = sub == 0

    def coefficients(cols, inside):
        for col in cols:
            r = jnp.broadcast_to(rext[pl.ds(col, 1), :], (8, 128))
            c = 1.0 / (1.0 / STEP + 4.0 + r)
            cp = c / STEP
            up = (1.0 / STEP + 4.0 + r) * STEP
            q2 = cp * cp
            q4 = q2 * q2
            q = q4 * q4
            qq = q * q
            qqqq = qq * qq
            cl = c * inside
            pw = inside
            for l in range(8):
                CL[col, part(l), :] = cl
                cl = cl * up
                if l:
                    pw = pw * cp
                    PW[col, part(l), :] = pw
            KS[col, part(0), :] = jnp.where(sub < 1, ALPHA * q, q)
            KS[col, part(1), :] = jnp.where(sub < 2, ALPHA * qq, qq)
            KS[col, part(2), :] = jnp.where(sub < 4, ALPHA * qqqq, qqqq)
            ks = inside * cp / (1.0 - ALPHA * (qqqq * qqqq))
            KS[col, part(3), :] = jnp.where(first, ALPHA * ks, ks)

    def solve(g, col):
        v = [g[0]]
        for l in range(1, 8):
            v.append(v[-1] + g[l])
        a = PW[col, part(7), :] * v[7]
        a = a + KS[col, part(0), :] * pltpu.roll(a, 1, 0)
        a = a + KS[col, part(1), :] * pltpu.roll(a, 2, 0)
        a = a + KS[col, part(2), :] * pltpu.roll(a, 4, 0)
        s = KS[col, part(3), :] * pltpu.roll(a, 1, 0)
        return [v[0] + s] + [PW[col, part(l), :] * (v[l] + s) for l in range(1, 8)]

    def rows_beside(v):
        return (jnp.where(lane == 0, 0.0, pltpu.roll(v, 1, 1))
                + jnp.where(lane == 127, 0.0, pltpu.roll(v, 127, 1)))

    def first_sweep(cols):
        done = []
        for col in cols:
            g = []
            for l in range(8):
                g.append(CL[col, part(l), :] * Rx[col, part(l), :])
            done.append((col, g, solve(g, col)))
        for col, g, u in done:
            for l in range(8):
                CR[col, part(l), :] = g[l]
                U0[col, part(l), :] = u[l]

    def around(U, col):
        return [
            (U[col - 1, part(l), :] + U[col + 1, part(l), :]) + rows_beside(U[col, part(l), :])
            for l in range(8)
        ]

    def at_corner(U, col):
        return jnp.where(first, CORNER * pltpu.roll(U[col, part(7), :], 1, 0), 0.0)

    def sweep(src, dst, cols, keep=False):
        done = []
        for col in cols:
            n = around(src, col)
            g = [CR[col, part(l), :] + CL[col, part(l), :] * n[l] for l in range(8)]
            done.append((col, n, solve(g, col)))
        for col, n, u in done:
            for l in range(8):
                dst[col, part(l), :] = u[l]
                if keep:
                    NB[col, part(l), :] = n[l]

    def turning_sweep(src, dst, cols, acc):
        done = []
        for col in cols:
            n = around(src, col)
            e = at_corner(src, col)
            c0 = CR[col, part(0), :] - CL[col, part(0), :] * e
            g = [c0 + CL[col, part(0), :] * n[0]]
            g += [CR[col, part(l), :] + CL[col, part(l), :] * n[l] for l in range(1, 8)]
            for l in range(8):
                r = n[l] - NB[col, part(l), :]
                if l == 0:
                    r = r - e
                acc = acc + r * r
            done.append((col, e, c0, solve(g, col)))
        for col, e, c0, u in done:
            E[col] = e
            CR[col, part(0), :] = c0
            for l in range(8):
                dst[col, part(l), :] = u[l]
        return acc

    def spread(lo, count, fn, carry=0, each=UNROLL):
        def step(i, carry):
            base = lo + each * i
            out = fn([base + k for k in range(each)], carry)
            return carry if out is None else out

        return lax.fori_loop(0, count // each, step, carry)

    spread(HALO, OWN, lambda cols, _: coefficients(cols, 1.0), each=1)
    mine.wait()
    for c in copies_a:
        c.wait()

    def unpack(cols, acc):
        for col in cols:
            rows = pl.ds(pl.multiple_of(8 * col, 8), 8)
            w = []
            for t in range(2):
                v = [rcv[4 * (s // 2) + 2 * t + s % 2, rows, :] for s in range(4)]
                w.append(swap_groups(v))
            for g in range(4):
                even = jnp.where(sub < 4, w[0][g], w[1][g])
                other = pltpu.roll(jnp.where(sub < 4, w[1][g], w[0][g]), 4, 0)
                Rx[HALO + col, part(2 * g), :] = even
                Rx[HALO + col, part(2 * g + 1), :] = other
                acc = acc + even * even + other * other
        return acc

    nothing = jnp.zeros((8, 128), jnp.float32)
    acc0 = spread(0, OWN, unpack, nothing, each=2)
    halo_r = halos(Rx, 1)
    for c in halo_r:
        c.start()
    spread(HALO, OWN, lambda cols, _: first_sweep(cols), each=2)

    def inner(j0, k, src, dst, keep=False):
        sweep(src, dst, [HALO + k + i for i in range(OWN - 2 * k)], keep)

    for i in range(3):
        inner(0, 2 * i + 1, U0, U1)
        inner(0, 2 * i + 2, U1, U0)
    inner(0, 7, U0, U1, True)

    for c in halo_c:
        c.wait()
    at_start = jnp.logical_and(sy == 0, d == 0)
    at_end = jnp.logical_and(sy == nsy - 1, d == 7)
    in_left = jnp.where(at_start, 0.0, 1.0)
    in_right = jnp.where(at_end, 0.0, 1.0)
    spread(0, HALO, lambda cols, _: coefficients(cols, in_left), each=1)
    spread(ENDS, HALO, lambda cols, _: coefficients(cols, in_right), each=1)
    for c in halo_r:
        c.wait()

    def strip(lo, way, src, dst, k, keep=False):
        spread(lo + way * k, HALO, lambda cols, _: sweep(src, dst, cols, keep))

    def strip_a(lo, way, acc):
        spread(0 if way > 0 else ENDS, HALO, lambda cols, _: first_sweep(cols), each=2)

        def pair(i, carry):
            strip(lo, way, U0, U1, 2 * i + 1)
            strip(lo, way, U1, U0, 2 * i + 2)
            return carry

        lax.fori_loop(0, 3, pair, 0)
        strip(lo, way, U0, U1, 7, True)
        return spread(lo + way * 8, HALO, lambda cols, a: turning_sweep(U1, V0, cols, a), acc)

    to_left, to_right = halos(V0, 2)
    e_left, e_right = halos(E, 3)
    acc1 = strip_a(0, 1, nothing)
    to_left.start()
    e_left.start()
    acc1 = strip_a(ENDS, -1, acc1)
    to_right.start()
    e_right.start()

    inner(9, 1, V0, U1)

    for i in range(2):
        inner(9, 2 * i + 2, U1, U0)
        inner(9, 2 * i + 3, U0, U1)
    inner(9, 6, U1, U0)
    inner(9, 7, U0, U1, True)

    def change_rhs(cols, _):
        for col in cols:
            CR[col, part(0), :] = CR[col, part(0), :] - CL[col, part(0), :] * E[col]

    def strip_b(lo, way, outside):
        @pl.when(outside)
        def _():
            def clear(cols, _):
                for col in cols:
                    V0[col] = jnp.zeros((64, 128), jnp.float32)

            spread(0 if way > 0 else ENDS, HALO, clear, each=1)

        spread(0 if way > 0 else ENDS, HALO, change_rhs)
        strip(lo, way, V0, U1, 1)

        def pair(i, carry):
            strip(lo, way, U1, U0, 2 * i + 2)
            strip(lo, way, U0, U1, 2 * i + 3)
            return carry

        lax.fori_loop(0, 2, pair, 0)
        strip(lo, way, U1, U0, 6)
        strip(lo, way, U0, U1, 7, True)

    to_left.wait()
    e_left.wait()
    strip_b(ENDS, -1, at_end)
    to_right.wait()
    e_right.wait()
    strip_b(0, 1, at_start)

    def left_over(cols, acc):
        for col in cols:
            n = around(U1, col)
            for l in range(8):
                r = n[l] - NB[col, part(l), :]
                if l == 0:
                    r = r + (E[col] - at_corner(U1, col))
                acc = acc + r * r
        return acc

    acc2 = spread(HALO, OWN, left_over, nothing, each=2)

    def total(v):
        return jnp.sum(v, axis=0, keepdims=True)

    redx[p] = jnp.where(sub == 0, total(acc0), jnp.where(sub == 1, total(acc1), jnp.where(
        sub == 2, total(acc2), 0.0)))
    copies_x = []
    for k in range(1, LINE):
        c = remote(redx.at[p], redx.at[p], x_s.at[k], x_r.at[k], in_line(lax.rem(p + k, LINE)))
        c.start()
        copies_x.append(c)

    def pack(cols, _):
        for col in cols:
            rows = pl.ds(pl.multiple_of(8 * col, 8), 8)
            w = [[], []]
            for g in range(4):
                even = U1[HALO + col, part(2 * g), :]
                other = pltpu.roll(U1[HALO + col, part(2 * g + 1), :], 4, 0)
                w[0].append(jnp.where(sub < 4, even, other))
                w[1].append(jnp.where(sub < 4, other, even))
            for t in range(2):
                v = swap_groups(w[t])
                for s in range(4):
                    M[4 * (s // 2) + 2 * t + s % 2, rows, :] = v[s]

    spread(0, OWN, pack, each=2)
    slot = pl.ds(pl.multiple_of(d * 128, 128), 128)
    copies_o = []
    for k in range(1, LINE):
        q = lax.rem(p + k, LINE)
        c = remote(M.at[q], O.at[slot], o_s.at[k], o_r.at[k], in_line(q))
        c.start()
        copies_o.append(c)
    mine = pltpu.make_async_copy(M.at[p], O.at[slot], l_s.at[1])
    mine.start()

    for c in copies_x:
        c.wait()
    sums = redx[0]
    for k in range(1, LINE):
        sums = sums + redx[k]
    if ny > 1:
        y = sy // nz
        redy[y] = sums
        copies_y = []
        for k in range(1, ny):
            c = remote(redy.at[y], redy.at[y], y_s.at[k], y_r.at[k], in_y(k))
            c.start()
            copies_y.append(c)
        for c in copies_y:
            c.wait()
        sums = redy[0]
        for k in range(1, ny):
            sums = sums + redy[k]
    if nz > 1:
        z = lax.rem(sy, nz)
        redz[z] = sums
        copies_z = []
        for k in range(1, nz):
            c = remote(redz.at[z], redz.at[z], z_s.at[k], z_r.at[k], in_z(k))
            c.start()
            copies_z.append(c)

    mine.wait()
    for c in copies_o:
        c.wait()
    for m in range(8):
        b = m % 4
        q = lax.rem(m // 4 + ta, 2)
        x = O[pl.ds(m, 128, stride=8), :].T
        for g in range(4):
            out[8 * b + 2 * g + q] = x[32 * g:32 * g + 32, :]

    if nz > 1:
        for c in copies_z:
            c.wait()
        sums = redz[0]
        for k in range(1, nz):
            sums = sums + redz[k]
    cells = 64.0 * 128.0 * (128.0 * nsy)
    for i in range(3):
        stat[i] = jnp.sum(sums[i:i + 1, :]) / cells


def solution(mesh):
    nsy = mesh.shape["sy"]
    ny, nz = (4, 8) if nsy == 32 else (2, nsy // 2)

    def step(forcing, react, initial):
        vmem = pl.BlockSpec(memory_space=pltpu.VMEM)
        dma = pltpu.SemaphoreType.DMA
        f32 = jnp.float32
        return pl.pallas_call(
            functools.partial(kernel, ny, nz),
            out_shape=(
                jax.ShapeDtypeStruct((32, 32, 128), f32),
                jax.ShapeDtypeStruct((3,), f32),
            ),
            in_specs=[pl.BlockSpec(memory_space=pltpu.HBM)] * 3,
            out_specs=(vmem, pl.BlockSpec(memory_space=pltpu.SMEM)),
            scratch_shapes=[
                pltpu.VMEM((32, 32, 128), f32),
                pltpu.VMEM((32, 128), f32),
                pltpu.VMEM((32, 128), f32),
                pltpu.VMEM((1024, 128), f32),
                pltpu.VMEM((8, 128, 128), f32),
                pltpu.VMEM((128, 128), f32),
                pltpu.VMEM((128, 128), f32),
                pltpu.VMEM((4, OWN, 128), f32),
                pltpu.VMEM((WIDE, 128), f32),
            ] + [pltpu.VMEM((WIDE, 64, 128), f32)] * 8 + [
                pltpu.VMEM((WIDE, 32, 128), f32),
                pltpu.VMEM((WIDE, 8, 128), f32),
                pltpu.VMEM((8, 128, 128), f32),
                pltpu.VMEM((1024, 128), f32),
                pltpu.VMEM((LINE, 8, 128), f32),
                pltpu.VMEM((max(ny, 2), 8, 128), f32),
                pltpu.VMEM((max(nz, 2), 8, 128), f32),
                dma((8,)), dma((8,)), dma((4,)), dma((4,)), dma((8,)), dma((8,)),
                dma((8,)), dma((8,)), dma((8,)), dma((8,)), dma((max(ny, 2),)),
                dma((max(ny, 2),)), dma((max(nz, 2),)), dma((max(nz, 2),)), dma((5,)),
            ],
            compiler_params=pltpu.CompilerParams(
                collective_id=0, has_side_effects=True, vmem_limit_bytes=48 << 20
            ),
        )(forcing, react, initial)

    placed = (P("ta", "sx", "sy"), P("sx", "sy"), P("sx", "sy"))
    return jax.shard_map(
        step, mesh=mesh, in_specs=placed, out_specs=(P("ta", "sx", "sy"), P(None)),
        check_vma=False,
    )
```

time: 103 us -> 53.7 us (0.52)
  Pallas kernels: 97.7 us -> 49 us
    pallas_call x1, Pallas kernels: 97.7 us -> 49 us  [step(): pl.pallas_call(functools.partial(kernel, ny, nz), out_shape=(jax.ShapeDty...]
where the time goes in v1:
time: 53.7 us; the launch traced here: 53.4 us
  Pallas kernels  49 us (91%)
  local copies, waits for them, and re-layouts  3.78 us (7%)
  between operations  0.65 us (1%)
    pallas_call x1, Pallas kernels, step(): pl.pallas_call(functools.partial(kernel, ny, nz), out_shape=(jax.ShapeDty...  49 us
    unnamed x8, local copies, waits for them, and re-layouts  3.78 us

profile of v1, /device:TPU:6, one launch (start us, length us, event | category | flops | bytes accessed | tf_op | source)
XLA Modules:
  0.0 53.4 jit_solution(15984565109464945905)
XLA Ops:
  0.6 0.0 copy-start
  0.6 1.0 %copy-done = f32[32,32,128]{2,1,0:T(8,128)S(1)} copy-done((f32[32,32,128]{2,1,0:T(8,128)S(1)}, f32[32,32,128]{2,1,0:T(8,128)}, u32[]{:S(2)}) %copy-start) | copy-done | bytes 524312
  1.7 0.0 copy-start.1
  1.7 0.7 %copy-done.1 = f32[32,128]{1,0:T(8,128)S(1)} copy-done((f32[32,128]{1,0:T(8,128)S(1)}, f32[32,128]{1,0:T(8,128)}, u32[]{:S(2)}) %copy-start.1) | copy-done | bytes 16408
  2.4 0.0 copy-start.2
  2.4 0.7 %copy-done.2 = f32[32,128]{1,0:T(8,128)S(1)} copy-done((f32[32,128]{1,0:T(8,128)S(1)}, f32[32,128]{1,0:T(8,128)}, u32[]{:S(2)}) %copy-start.2) | copy-done | bytes 16408
  3.1 49.0 %shard_map.50 = (f32[32,32,128]{2,1,0:T(8,128)S(1)}, f32[3]{0:T(128)S(1)}) custom-call(f32[32,32,128]{2,1,0:T(8,128)S(1)} %copy-done, f32[32,128]{1,0:T(8,128)S(1)} %copy-done.1, f32[32,128]{1,0:T(8,128)S(1)} %copy-done.2), custom_call_target="tpu_custom_call" | custom-call | tf_op jit(solution)/shard_map/pallas_call | solution.py:482
  52.1 0.8 %copy.7 = f32[32,32,128]{2,1,0:T(8,128)} copy(f32[32,32,128]{2,1,0:T(8,128)S(1)} %get-tuple-element.4) | data formatting | bytes 1048576
  52.9 0.5 copy.8
Async XLA Ops:
  0.6 1.0 %copy-start = (f32[32,32,128]{2,1,0:T(8,128)S(1)}, f32[32,32,128]{2,1,0:T(8,128)}, u32[]{:S(2)}) copy-start(f32[32,32,128]{2,1,0:T(8,128)} %f_hbm.1) | copy-start | bytes 1572868
  1.7 0.7 %copy-start.1 = (f32[32,128]{1,0:T(8,128)S(1)}, f32[32,128]{1,0:T(8,128)}, u32[]{:S(2)}) copy-start(f32[32,128]{1,0:T(8,128)} %react_hbm.1) | copy-start | bytes 49156
  2.4 0.7 %copy-start.2 = (f32[32,128]{1,0:T(8,128)S(1)}, f32[32,128]{1,0:T(8,128)}, u32[]{:S(2)}) copy-start(f32[32,128]{1,0:T(8,128)} %init_hbm.1) | copy-start | bytes 49156

commit v2 on v1

--- a/solution.py
+++ b/solution.py
@@ -16,6 +16,7 @@
 WIDE = OWN + 2 * HALO
 ENDS = HALO + OWN
 LINE = 8
+HUB = LINE - 1
 UNROLL = 8
 MESH = pl.DeviceIdType.MESH
 
@@ -51,8 +52,8 @@
 
 
 def kernel(ny, nz, f_hbm, react_hbm, init_hbm, out, stat, f, react, init, S, rcv, tmp, rsend, rrecv,
-           rext, Rx, CR, U0, U1, V0, NB, CL, PW, KS, E, M, O, redx, redy, redz, a_s, a_r, c_s, c_r,
-           h_s, h_r, o_s, o_r, x_s, x_r, y_s, y_r, z_s, z_r, l_s):
+           rext, Rx, CR, U0, U1, V0, NB, CL, PW, KS, E, M, O, redx, redz, a_s, a_r, c_s, c_r,
+           h_s, h_r, o_s, o_r, x_s, x_r, z_s, z_r, l_s, near, far):
     sx, sy, ta = lax.axis_index("sx"), lax.axis_index("sy"), lax.axis_index("ta")
     nsy = ny * nz
     p = 4 * (sx // 2) + 2 * ta + sx % 2
@@ -75,28 +76,25 @@
         a, b = place_of(e)
         return {"sx": a, "sy": s, "ta": b}
 
-    def in_y(k):
-        return {"sx": sx, "sy": lax.rem(sy + nz * k, nsy), "ta": ta}
-
-    def in_z(k):
-        z = lax.rem(sy, nz)
-        return {"sx": sx, "sy": sy - z + lax.rem(z + k, nz), "ta": ta}
+    def in_plane(k):
+        return {"sx": sx, "sy": lax.rem(sy + k, nsy), "ta": ta}
 
     left, right = beside(-1), beside(1)
     inputs = [
-        pltpu.make_async_copy(react_hbm, react, l_s.at[2]),
-        pltpu.make_async_copy(init_hbm, init, l_s.at[3]),
-        pltpu.make_async_copy(f_hbm, f, l_s.at[4]),
+        pltpu.make_async_copy(react_hbm, react, l_s.at[4]),
+        pltpu.make_async_copy(init_hbm, init, l_s.at[5]),
+        pltpu.make_async_copy(f_hbm, f, l_s.at[6]),
     ]
     for c in inputs:
         c.start()
     barrier = pltpu.get_barrier_semaphore()
-    peers = [in_line(lax.rem(p + k, LINE)) for k in range(1, LINE)]
-    peers += [left, right]
-    peers += [in_y(k) for k in range(1, ny)]
-    peers += [in_z(k) for k in range(1, nz)]
-    for peer in peers:
-        pl.semaphore_signal(barrier, inc=1, device_id=peer, device_id_type=MESH)
+    hub = p == HUB
+    for k in range(1, LINE):
+        q = lax.rem(p + k, LINE)
+
+        @pl.when(q != HUB)
+        def _():
+            pl.semaphore_signal(barrier, inc=1, device_id=in_line(q), device_id_type=MESH)
 
     def remote(src, dst, s_sem, r_sem, peer):
         return pltpu.make_async_remote_copy(
@@ -119,7 +117,24 @@
             planes[0] = planes[0] + opening * init[...]
         S[pl.ds(m, 128, stride=8), :] = jnp.concatenate(planes, axis=0).T
 
-    pl.semaphore_wait(barrier, len(peers))
+    @pl.when(jnp.logical_not(hub))
+    def _():
+        pl.semaphore_wait(barrier, LINE - 1)
+
+    @pl.when(p == HUB - 1)
+    def _():
+        pl.semaphore_signal(near, inc=1, device_id=in_line(HUB), device_id_type=MESH)
+
+    @pl.when(hub)
+    def _():
+        pl.semaphore_wait(near, 1)
+
+        def greet(k, carry):
+            pl.semaphore_signal(barrier, inc=1, device_id=in_plane(k), device_id_type=MESH)
+            return carry
+
+        lax.fori_loop(1, nsy, greet, 0)
+
 
     copies_c = []
     for k in range(1, 4):
@@ -130,16 +145,21 @@
                    {"sx": to, "sy": sy, "ta": ta})
         c.start()
         copies_c.append(c)
-    copies_a = []
-    for k in range(1, LINE):
-        q = lax.rem(p + k, LINE)
-        rows = pl.ds(pl.multiple_of(slice_of(q) * 128, 128), 128)
-        c = remote(S.at[rows], rcv.at[p], a_s.at[k], a_r.at[k], in_line(q))
-        c.start()
-        copies_a.append(c)
-    mine = pltpu.make_async_copy(S.at[pl.ds(pl.multiple_of(d * 128, 128), 128)], rcv.at[p],
-                                 l_s.at[0])
-    mine.start()
+    copies_a = [[], []]
+    for h in range(2):
+        slots = pl.ds(64 * h, 64)
+
+        def rows_of(q):
+            return pl.ds(pl.multiple_of(slice_of(q) * 128 + 64 * h, 64), 64)
+
+        for k in range(1, LINE):
+            q = lax.rem(p + k, LINE)
+            copies_a[h].append(remote(S.at[rows_of(q)], rcv.at[p, slots], a_s.at[8 * h + k],
+                                      a_r.at[8 * h + k], in_line(q)))
+        copies_a[h].append(
+            pltpu.make_async_copy(S.at[rows_of(p)], rcv.at[p, slots], l_s.at[h]))
+        for c in copies_a[h]:
+            c.start()
     rrecv[sx] = rsend[pl.ds(pl.multiple_of(d * OWN, OWN), OWN), :]
     for c in copies_c:
         c.wait()
@@ -156,8 +176,6 @@
         return edges(ref, ref.at[pl.ds(ENDS, HALO)], ref.at[pl.ds(0, HALO)], k)
 
     halo_c = halos(rext, 0)
-    for c in halo_c:
-        c.start()
 
     sub = iota(0)
     lane = iota(1)
@@ -266,9 +284,13 @@
         return lax.fori_loop(0, count // each, step, carry)
 
     spread(HALO, OWN, lambda cols, _: coefficients(cols, 1.0), each=1)
-    mine.wait()
-    for c in copies_a:
-        c.wait()
+
+    @pl.when(hub)
+    def _():
+        pl.semaphore_wait(barrier, nsy - 1)
+        for q in range(LINE - 1):
+            pl.semaphore_signal(far, inc=1, device_id=in_line(q), device_id_type=MESH)
+
 
     def unpack(cols, acc):
         for col in cols:
@@ -286,10 +308,20 @@
         return acc
 
     nothing = jnp.zeros((8, 128), jnp.float32)
-    acc0 = spread(0, OWN, unpack, nothing, each=2)
     halo_r = halos(Rx, 1)
-    for c in halo_r:
-        c.start()
+    acc0 = nothing
+    for h in range(2):
+        for c in copies_a[h]:
+            c.wait()
+        acc0 = spread(HALO * h, HALO, unpack, acc0, each=2)
+        if h == 0:
+            @pl.when(jnp.logical_not(hub))
+            def _():
+                pl.semaphore_wait(far, 1)
+
+            for c in halo_c:
+                c.start()
+        halo_r[h].start()
     spread(HALO, OWN, lambda cols, _: first_sweep(cols), each=2)
 
     def inner(j0, k, src, dst, keep=False):
@@ -368,13 +400,6 @@
         strip(lo, way, U1, U0, 6)
         strip(lo, way, U0, U1, 7, True)
 
-    to_left.wait()
-    e_left.wait()
-    strip_b(ENDS, -1, at_end)
-    to_right.wait()
-    e_right.wait()
-    strip_b(0, 1, at_start)
-
     def left_over(cols, acc):
         for col in cols:
             n = around(U1, col)
@@ -385,18 +410,6 @@
                 acc = acc + r * r
         return acc
 
-    acc2 = spread(HALO, OWN, left_over, nothing, each=2)
-
-    def total(v):
-        return jnp.sum(v, axis=0, keepdims=True)
-
-    redx[p] = jnp.where(sub == 0, total(acc0), jnp.where(sub == 1, total(acc1), jnp.where(
-        sub == 2, total(acc2), 0.0)))
-    copies_x = []
-    for k in range(1, LINE):
-        c = remote(redx.at[p], redx.at[p], x_s.at[k], x_r.at[k], in_line(lax.rem(p + k, LINE)))
-        c.start()
-        copies_x.append(c)
 
     def pack(cols, _):
         for col in cols:
@@ -412,45 +425,59 @@
                 for s in range(4):
                     M[4 * (s // 2) + 2 * t + s % 2, rows, :] = v[s]
 
-    spread(0, OWN, pack, each=2)
-    slot = pl.ds(pl.multiple_of(d * 128, 128), 128)
     copies_o = []
+
+    def send_out(h):
+        slot = pl.ds(pl.multiple_of(d * 128 + 64 * h, 64), 64)
+        rows = pl.ds(64 * h, 64)
+        for k in range(1, LINE):
+            q = lax.rem(p + k, LINE)
+            copies_o.append(remote(M.at[q, rows], O.at[slot], o_s.at[8 * h + k],
+                                   o_r.at[8 * h + k], in_line(q)))
+            copies_o[-1].start()
+        copies_o.append(pltpu.make_async_copy(M.at[p, rows], O.at[slot], l_s.at[2 + h]))
+        copies_o[-1].start()
+
+    to_left.wait()
+    e_left.wait()
+    strip_b(ENDS, -1, at_end)
+    acc2 = spread(HALO + OWN // 2, OWN // 2, left_over, nothing, each=4)
+    spread(OWN // 2, OWN // 2, pack, each=2)
+    send_out(1)
+    to_right.wait()
+    e_right.wait()
+    strip_b(0, 1, at_start)
+    acc2 = spread(HALO, OWN // 2, left_over, acc2, each=4)
+
+    def total(v):
+        return jnp.sum(v, axis=0, keepdims=True)
+
+    redx[p] = jnp.where(sub == 0, total(acc0), jnp.where(sub == 1, total(acc1), jnp.where(
+        sub == 2, total(acc2), 0.0)))
+    copies_x = []
     for k in range(1, LINE):
-        q = lax.rem(p + k, LINE)
-        c = remote(M.at[q], O.at[slot], o_s.at[k], o_r.at[k], in_line(q))
+        c = remote(redx.at[p], redx.at[p], x_s.at[k], x_r.at[k], in_line(lax.rem(p + k, LINE)))
         c.start()
-        copies_o.append(c)
-    mine = pltpu.make_async_copy(M.at[p], O.at[slot], l_s.at[1])
-    mine.start()
-
+        copies_x.append(c)
+
+    spread(0, OWN // 2, pack, each=2)
+    send_out(0)
     for c in copies_x:
         c.wait()
     sums = redx[0]
     for k in range(1, LINE):
         sums = sums + redx[k]
-    if ny > 1:
-        y = sy // nz
-        redy[y] = sums
-        copies_y = []
-        for k in range(1, ny):
-            c = remote(redy.at[y], redy.at[y], y_s.at[k], y_r.at[k], in_y(k))
-            c.start()
-            copies_y.append(c)
-        for c in copies_y:
-            c.wait()
-        sums = redy[0]
-        for k in range(1, ny):
-            sums = sums + redy[k]
-    if nz > 1:
-        z = lax.rem(sy, nz)
-        redz[z] = sums
-        copies_z = []
-        for k in range(1, nz):
-            c = remote(redz.at[z], redz.at[z], z_s.at[k], z_r.at[k], in_z(k))
-            c.start()
-            copies_z.append(c)
-
-    mine.wait()
+    redz[sy] = sums
+
+    def plane(k):
+        return remote(redz.at[sy], redz.at[sy], z_s.at[k], z_r.at[k], in_plane(k))
+
+    def send(k, carry):
+        plane(k).start()
+        return carry
+
+    lax.fori_loop(1, nsy, send, 0)
+
     for c in copies_o:
         c.wait()
     for m in range(8):
@@ -460,12 +487,14 @@
         for g in range(4):
             out[8 * b + 2 * g + q] = x[32 * g:32 * g + 32, :]
 
-    if nz > 1:
-        for c in copies_z:
-            c.wait()
-        sums = redz[0]
-        for k in range(1, nz):
-            sums = sums + redz[k]
+    def arrive(k, carry):
+        plane(k).wait()
+        return carry
+
+    lax.fori_loop(1, nsy, arrive, 0)
+    sums = redz[0]
+    for k in range(1, nsy):
+        sums = sums + redz[k]
     cells = 64.0 * 128.0 * (128.0 * nsy)
     for i in range(3):
         stat[i] = jnp.sum(sums[i:i + 1, :]) / cells
@@ -503,14 +532,14 @@
                 pltpu.VMEM((8, 128, 128), f32),
                 pltpu.VMEM((1024, 128), f32),
                 pltpu.VMEM((LINE, 8, 128), f32),
-                pltpu.VMEM((max(ny, 2), 8, 128), f32),
-                pltpu.VMEM((max(nz, 2), 8, 128), f32),
-                dma((8,)), dma((8,)), dma((4,)), dma((4,)), dma((8,)), dma((8,)),
-                dma((8,)), dma((8,)), dma((8,)), dma((8,)), dma((max(ny, 2),)),
-                dma((max(ny, 2),)), dma((max(nz, 2),)), dma((max(nz, 2),)), dma((5,)),
+                pltpu.VMEM((ny * nz, 8, 128), f32),
+                dma((16,)), dma((16,)), dma((4,)), dma((4,)), dma((8,)), dma((8,)),
+                dma((16,)), dma((16,)), dma((8,)), dma((8,)),
+                dma((ny * nz,)), dma((ny * nz,)), dma((7,)),
+                pltpu.SemaphoreType.REGULAR, pltpu.SemaphoreType.REGULAR,
             ],
             compiler_params=pltpu.CompilerParams(
-                collective_id=0, has_side_effects=True, vmem_limit_bytes=48 << 20
+                collective_id=0, has_side_effects=True, vmem_limit_bytes=67043328
             ),
         )(forcing, react, initial)
 

time: 53.7 us -> 50.5 us (0.940); the launches traced: 53.4 us -> 49.6 us
  Pallas kernels: 49 us -> 46.5 us
  local copies, waits for them, and re-layouts: 3.78 us -> 2.38 us
    pallas_call x1, Pallas kernels: 49 us -> 46.5 us  [step(): pl.pallas_call(functools.partial(kernel, ny, nz), out_shape=(jax.ShapeDty...]
    unnamed x8 -> x4, local copies, waits for them, and re-layouts: 3.78 us -> 2.38 us
where the time goes in v2:
time: 50.5 us; the launch traced here: 49.6 us
  Pallas kernels  46.5 us (92%)
  local copies, waits for them, and re-layouts  2.38 us (5%)
  between operations  0.65 us (1%)
    pallas_call x1, Pallas kernels, step(): pl.pallas_call(functools.partial(kernel, ny, nz), out_shape=(jax.ShapeDty...  46.5 us
    unnamed x4, local copies, waits for them, and re-layouts  2.38 us

profile of v2, /device:TPU:6, one launch (start us, length us, event | category | flops | bytes accessed | tf_op | source)
XLA Modules:
  0.0 49.6 jit_solution(4832500962979216167)
XLA Ops:
  0.6 46.5 %shard_map.50 = (f32[32,32,128]{2,1,0:T(8,128)}, f32[3]{0:T(128)}) custom-call(f32[32,32,128]{2,1,0:T(8,128)} %f_hbm.1, f32[32,128]{1,0:T(8,128)} %react_hbm.1, f32[32,128]{1,0:T(8,128)} %init_hbm.1), custom_call_target="tpu_custom_call" | custom-call | tf_op jit(solution)/shard_map/pallas_call | solution.py:511
  47.2 0.0 copy-start
  47.2 1.9 %copy.7 = f32[32,32,128]{2,1,0:T(8,128)} copy(f32[32,32,128]{2,1,0:T(8,128)} %get-tuple-element.4) | data formatting | bytes 1048576
  49.1 0.0 copy-done
  49.1 0.5 %copy.8 = f32[3]{0:T(128)} copy(f32[3]{0:T(128)S(1)} %copy-done) | data formatting | bytes 24
Async XLA Ops:
  47.2 1.9 %copy-start = (f32[3]{0:T(128)S(1)}, f32[3]{0:T(128)}, u32[]{:S(2)}) copy-start(f32[3]{0:T(128)} %get-tuple-element.5) | copy-start | bytes 40

commit v3 on v2

--- a/solution.py
+++ b/solution.py
@@ -18,6 +18,7 @@
 LINE = 8
 HUB = LINE - 1
 UNROLL = 8
+TURN_VMEM = 67043328
 MESH = pl.DeviceIdType.MESH
 
 
@@ -33,12 +34,14 @@
     lane = iota(1)
     low = lane < 64
     even = (lane // 32) % 2 == 0
-    a = [
-        jnp.where(low, v[0], pltpu.roll(v[2], 64, 1)),
-        jnp.where(low, v[1], pltpu.roll(v[3], 64, 1)),
-        jnp.where(low, pltpu.roll(v[0], 64, 1), v[2]),
-        jnp.where(low, pltpu.roll(v[1], 64, 1), v[3]),
-    ]
+
+    def cross(a, b):
+        y = pltpu.roll(jnp.where(low, b, a), 64, 1)
+        return jnp.where(low, a, y), jnp.where(low, y, b)
+
+    a0, a2 = cross(v[0], v[2])
+    a1, a3 = cross(v[1], v[3])
+    a = [a0, a1, a2, a3]
     return [
         jnp.where(even, a[0], pltpu.roll(a[1], 32, 1)),
         jnp.where(even, pltpu.roll(a[0], 96, 1), a[1]),
@@ -51,8 +54,8 @@
     return pl.ds(8 * l, 8)
 
 
-def kernel(ny, nz, f_hbm, react_hbm, init_hbm, out, stat, f, react, init, S, rcv, tmp, rsend, rrecv,
-           rext, Rx, CR, U0, U1, V0, NB, CL, PW, KS, E, M, O, redx, redz, a_s, a_r, c_s, c_r,
+def kernel(ny, nz, f_hbm, react_hbm, init_hbm, O, stat, f, react, init, S, rcv, tmp, rsend, rrecv,
+           rext, Rx, CR, U0, U1, V0, NB, CL, PW, KS, E, M, redx, redz, a_s, a_r, c_s, c_r,
            h_s, h_r, o_s, o_r, x_s, x_r, z_s, z_r, l_s, near, far):
     sx, sy, ta = lax.axis_index("sx"), lax.axis_index("sy"), lax.axis_index("ta")
     nsy = ny * nz
@@ -332,16 +335,10 @@
         inner(0, 2 * i + 2, U1, U0)
     inner(0, 7, U0, U1, True)
 
-    for c in halo_c:
-        c.wait()
     at_start = jnp.logical_and(sy == 0, d == 0)
     at_end = jnp.logical_and(sy == nsy - 1, d == 7)
     in_left = jnp.where(at_start, 0.0, 1.0)
     in_right = jnp.where(at_end, 0.0, 1.0)
-    spread(0, HALO, lambda cols, _: coefficients(cols, in_left), each=1)
-    spread(ENDS, HALO, lambda cols, _: coefficients(cols, in_right), each=1)
-    for c in halo_r:
-        c.wait()
 
     def strip(lo, way, src, dst, k, keep=False):
         spread(lo + way * k, HALO, lambda cols, _: sweep(src, dst, cols, keep))
@@ -360,12 +357,18 @@
 
     to_left, to_right = halos(V0, 2)
     e_left, e_right = halos(E, 3)
-    acc1 = strip_a(0, 1, nothing)
+    halo_c[0].wait()
+    spread(ENDS, HALO, lambda cols, _: coefficients(cols, in_right), each=1)
+    halo_r[0].wait()
+    acc1 = strip_a(ENDS, -1, nothing)
+    to_right.start()
+    e_right.start()
+    halo_c[1].wait()
+    spread(0, HALO, lambda cols, _: coefficients(cols, in_left), each=1)
+    halo_r[1].wait()
+    acc1 = strip_a(0, 1, acc1)
     to_left.start()
     e_left.start()
-    acc1 = strip_a(ENDS, -1, acc1)
-    to_right.start()
-    e_right.start()
 
     inner(9, 1, V0, U1)
 
@@ -438,16 +441,16 @@
         copies_o.append(pltpu.make_async_copy(M.at[p, rows], O.at[slot], l_s.at[2 + h]))
         copies_o[-1].start()
 
+    to_right.wait()
+    e_right.wait()
+    strip_b(0, 1, at_start)
+    acc2 = spread(HALO, OWN // 2, left_over, nothing, each=4)
+    spread(0, OWN // 2, pack, each=2)
+    send_out(0)
     to_left.wait()
     e_left.wait()
     strip_b(ENDS, -1, at_end)
-    acc2 = spread(HALO + OWN // 2, OWN // 2, left_over, nothing, each=4)
-    spread(OWN // 2, OWN // 2, pack, each=2)
-    send_out(1)
-    to_right.wait()
-    e_right.wait()
-    strip_b(0, 1, at_start)
-    acc2 = spread(HALO, OWN // 2, left_over, acc2, each=4)
+    acc2 = spread(HALO + OWN // 2, OWN // 2, left_over, acc2, each=4)
 
     def total(v):
         return jnp.sum(v, axis=0, keepdims=True)
@@ -460,8 +463,8 @@
         c.start()
         copies_x.append(c)
 
-    spread(0, OWN // 2, pack, each=2)
-    send_out(0)
+    spread(OWN // 2, OWN // 2, pack, each=2)
+    send_out(1)
     for c in copies_x:
         c.wait()
     sums = redx[0]
@@ -480,13 +483,6 @@
 
     for c in copies_o:
         c.wait()
-    for m in range(8):
-        b = m % 4
-        q = lax.rem(m // 4 + ta, 2)
-        x = O[pl.ds(m, 128, stride=8), :].T
-        for g in range(4):
-            out[8 * b + 2 * g + q] = x[32 * g:32 * g + 32, :]
-
     def arrive(k, carry):
         plane(k).wait()
         return carry
@@ -495,7 +491,17 @@
     sums = redz[0]
     for k in range(1, nsy):
         sums = sums + redz[k]
-    cells = 64.0 * 128.0 * (128.0 * nsy)
+    stat[...] = sums
+
+
+def turn(cells, turned, sums, out, stat):
+    ta = lax.axis_index("ta")
+    for m in range(8):
+        b = m % 4
+        q = lax.rem(m // 4 + ta, 2)
+        x = turned[pl.ds(m, 128, stride=8), :].T
+        for g in range(4):
+            out[8 * b + 2 * g + q] = x[32 * g:32 * g + 32, :]
     for i in range(3):
         stat[i] = jnp.sum(sums[i:i + 1, :]) / cells
 
@@ -508,14 +514,14 @@
         vmem = pl.BlockSpec(memory_space=pltpu.VMEM)
         dma = pltpu.SemaphoreType.DMA
         f32 = jnp.float32
-        return pl.pallas_call(
+        turned, sums = pl.pallas_call(
             functools.partial(kernel, ny, nz),
             out_shape=(
-                jax.ShapeDtypeStruct((32, 32, 128), f32),
-                jax.ShapeDtypeStruct((3,), f32),
+                jax.ShapeDtypeStruct((1024, 128), f32),
+                jax.ShapeDtypeStruct((8, 128), f32),
             ),
             in_specs=[pl.BlockSpec(memory_space=pltpu.HBM)] * 3,
-            out_specs=(vmem, pl.BlockSpec(memory_space=pltpu.SMEM)),
+            out_specs=(pl.BlockSpec(memory_space=pltpu.HBM), vmem),
             scratch_shapes=[
                 pltpu.VMEM((32, 32, 128), f32),
                 pltpu.VMEM((32, 128), f32),
@@ -530,7 +536,6 @@
                 pltpu.VMEM((WIDE, 32, 128), f32),
                 pltpu.VMEM((WIDE, 8, 128), f32),
                 pltpu.VMEM((8, 128, 128), f32),
-                pltpu.VMEM((1024, 128), f32),
                 pltpu.VMEM((LINE, 8, 128), f32),
                 pltpu.VMEM((ny * nz, 8, 128), f32),
                 dma((16,)), dma((16,)), dma((4,)), dma((4,)), dma((8,)), dma((8,)),
@@ -542,6 +547,16 @@
                 collective_id=0, has_side_effects=True, vmem_limit_bytes=67043328
             ),
         )(forcing, react, initial)
+        return pl.pallas_call(
+            functools.partial(turn, 64.0 * 128.0 * 128.0 * nsy),
+            out_shape=(
+                jax.ShapeDtypeStruct((32, 32, 128), f32),
+                jax.ShapeDtypeStruct((3,), f32),
+            ),
+            in_specs=[vmem] * 2,
+            out_specs=(vmem, pl.BlockSpec(memory_space=pltpu.SMEM)),
+            compiler_params=pltpu.CompilerParams(vmem_limit_bytes=TURN_VMEM),
+        )(turned, sums)
 
     placed = (P("ta", "sx", "sy"), P("sx", "sy"), P("sx", "sy"))
     return jax.shard_map(

time: 50.5 us -> 48.4 us (0.958); the launches traced: 49.6 us -> 48.2 us
  local copies, waits for them, and re-layouts: 2.38 us -> 0 us
  Pallas kernels: 46.5 us -> 47.5 us
    unnamed x4 -> x0, local copies, waits for them, and re-layouts: 2.38 us -> none
    pallas_call x0 -> x1, Pallas kernels: none -> 2.09 us  [step(): pl.pallas_call(functools.partial(turn, 64.0 * 128.0 * 128.0 * nsy), out_s...]
    pallas_call x1, Pallas kernels: 46.5 us -> 45.4 us  [step(): pl.pallas_call(functools.partial(kernel, ny, nz), out_shape=(jax.ShapeDty...]
where the time goes in v3:
time: 48.4 us; the launch traced here: 48.2 us
  Pallas kernels  47.5 us (98%)
  between operations  0.64 us (1%)
    pallas_call x1, Pallas kernels, step(): pl.pallas_call(functools.partial(kernel, ny, nz), out_shape=(jax.ShapeDty...  45.4 us
    pallas_call x1, Pallas kernels, step(): pl.pallas_call(functools.partial(turn, 64.0 * 128.0 * 128.0 * nsy), out_s...  2.09 us

profile of v3, /device:TPU:6, one launch (start us, length us, event | category | flops | bytes accessed | tf_op | source)
XLA Modules:
  0.0 48.2 jit_solution(5347647729373908628)
XLA Ops:
  0.6 45.4 %shard_map.50 = (f32[1024,128]{1,0:T(8,128)}, f32[8,128]{1,0:T(8,128)}) custom-call(f32[32,32,128]{2,1,0:T(8,128)} %f_hbm.1, f32[32,128]{1,0:T(8,128)} %react_hbm.1, f32[32,128]{1,0:T(8,128)} %init_hbm.1), custom_call_target="tpu_custom_call" | custom-call | tf_op jit(solution)/shard_map/pallas_call | solution.py:517
  46.1 2.1 %shard_map.51 = (f32[32,32,128]{2,1,0:T(8,128)}, f32[3]{0:T(128)}) custom-call(f32[1024,128]{1,0:T(8,128)} %get-tuple-element.4.turned, f32[8,128]{1,0:T(8,128)} %get-tuple-element.5.sums), custom_call_target="tpu_custom_call" | custom-call | tf_op jit(solution)/shard_map/pallas_call | solution.py:550

commit v4 on v3

--- a/solution.py
+++ b/solution.py
@@ -494,16 +494,22 @@
     stat[...] = sums
 
 
-def turn(cells, turned, sums, out, stat):
+def turn(cells, turned, sums, out, stat, done, o_s):
     ta = lax.axis_index("ta")
+    copies = []
     for m in range(8):
         b = m % 4
         q = lax.rem(m // 4 + ta, 2)
         x = turned[pl.ds(m, 128, stride=8), :].T
         for g in range(4):
-            out[8 * b + 2 * g + q] = x[32 * g:32 * g + 32, :]
+            done[m, g] = x[32 * g:32 * g + 32, :]
+            copies.append(pltpu.make_async_copy(
+                done.at[m, g], out.at[8 * b + 2 * g + q], o_s.at[4 * m + g]))
+            copies[-1].start()
     for i in range(3):
         stat[i] = jnp.sum(sums[i:i + 1, :]) / cells
+    for c in copies:
+        c.wait()
 
 
 def solution(mesh):
@@ -554,7 +560,8 @@
                 jax.ShapeDtypeStruct((3,), f32),
             ),
             in_specs=[vmem] * 2,
-            out_specs=(vmem, pl.BlockSpec(memory_space=pltpu.SMEM)),
+            out_specs=(pl.BlockSpec(memory_space=pltpu.HBM), pl.BlockSpec(memory_space=pltpu.SMEM)),
+            scratch_shapes=[pltpu.VMEM((8, 4, 32, 128), f32), dma((32,))],
             compiler_params=pltpu.CompilerParams(vmem_limit_bytes=TURN_VMEM),
         )(turned, sums)
 

time: 48.4 us -> 49 us (1.012)
  Pallas kernels: 47.5 us -> 48.2 us
    pallas_call x1, Pallas kernels: 2.09 us -> 2.72 us  [step(): pl.pallas_call(functools.partial(turn, 64.0 * 128.0 * 128.0 * nsy), out_s...]
where the time goes in v4:
time: 49 us; the launch traced here: 48.8 us
  Pallas kernels  48.2 us (98%)
  between operations  0.64 us (1%)
    pallas_call x1, Pallas kernels, step(): pl.pallas_call(functools.partial(kernel, ny, nz), out_shape=(jax.ShapeDty...  45.4 us
    pallas_call x1, Pallas kernels, step(): pl.pallas_call(functools.partial(turn, 64.0 * 128.0 * 128.0 * nsy), out_s...  2.72 us

profile of v4, /device:TPU:6, one launch (start us, length us, event | category | flops | bytes accessed | tf_op | source)
XLA Modules:
  0.0 48.8 jit_solution(1791504494073359953)
XLA Ops:
  0.6 45.4 %shard_map.50 = (f32[1024,128]{1,0:T(8,128)}, f32[8,128]{1,0:T(8,128)}) custom-call(f32[32,32,128]{2,1,0:T(8,128)} %f_hbm.1, f32[32,128]{1,0:T(8,128)} %react_hbm.1, f32[32,128]{1,0:T(8,128)} %init_hbm.1), custom_call_target="tpu_custom_call" | custom-call | tf_op jit(solution)/shard_map/pallas_call | solution.py:523
  46.1 2.7 %shard_map.51 = (f32[32,32,128]{2,1,0:T(8,128)}, f32[3]{0:T(128)}) custom-call(f32[1024,128]{1,0:T(8,128)} %get-tuple-element.4.turned, f32[8,128]{1,0:T(8,128)} %get-tuple-element.5.sums), custom_call_target="tpu_custom_call" | custom-call | tf_op jit(solution)/shard_map/pallas_call | solution.py:556
